TPU v7x, 32 devices: a whole 2x2x4 slice. The times are simulated.
32 devices in a mesh: groups: 2 (over y), tile: 4 (over z), image: 4 (over x, core).
Axes of the slice: x: 2, y: 2, z: 4, core: 2. Of those that a mesh axis runs over, the one named last changes fastest.
Arguments:
- images: bfloat16 [8, 16, 64, 256], P(('groups', 'image'), 'tile'), parts along dimension 0, may hold values from -12 to 12
- cotangent: bfloat16 [8, 16, 64, 256], P(('groups', 'image'), 'tile'), parts along dimension 0, may hold values from -12 to 12
- timesteps: int32 [8], P(('groups', 'image')), parts along dimension 0, may hold values from 0 to 999
- class_ids: int32 [8], P(('groups', 'image')), parts along dimension 0, may hold values from 0 to 999
- norm_gain: float32 [256], replicated, may hold values from 0.25 to 1.75
- norm_bias: float32 [256], replicated, may hold values from -3 to 3
- conv_first: bfloat16 [3, 3, 256, 256], replicated, may hold values from -0.125 to 0.125
- conv_second: bfloat16 [3, 3, 256, 256], replicated, may hold values from -0.125 to 0.125
- time_weight: bfloat16 [256, 1024], P(None, 'tile'), may hold values from -0.375 to 0.375
- time_bias: float32 [1024], P('tile'), may hold values from -3 to 3
- class_table: bfloat16 [1000, 1024], P(None, 'tile'), may hold values from -5 to 5
- adaptive_weight: bfloat16 [1024, 512], P('tile'), may hold values from -0.1875 to 0.1875
- adaptive_bias: float32 [512], replicated, may hold values from -2 to 2
Outputs:
- branch: bfloat16 [8, 16, 64, 256], P(('groups', 'image'), 'tile'), parts along dimension 0
- input_grad: bfloat16 [8, 16, 64, 256], P(('groups', 'image'), 'tile'), parts along dimension 0
- grad_adaptive_weight: float32 [2048, 512], P(('groups', 'tile')), parts along dimension 0
- grad_adaptive_bias: float32 [1024], P('groups'), parts along dimension 0
There are 2 independent parts, one for each index of `groups`. A program takes and returns all parts, laid end to end along the dimension named above; an argument that names none is the same for every part. Nothing has to cross between parts.
All inputs are finite; a program needn't handle non-finite values.
Results may differ from a plain program's by a relative error of at most 0.013.
Values may be sent and summed in bfloat16 or wider, within the bound.
A program may use at most 64 MiB of HBM per device.

v0:
```python
import math

import jax
import jax.numpy as jnp
from jax import lax
from jax.sharding import PartitionSpec as P

GN_GROUPS = 32


EPSILON = 1e-05


def with_halo(block, sides, width):
    for axis, dim in sides:
        count = lax.axis_size(axis)
        forward = [(i, i + 1) for i in range(count - 1)]
        backward = [(target, source) for source, target in forward]
        low = lax.ppermute(
            lax.slice_in_dim(block, block.shape[dim] - width, None, axis=dim), axis, forward
        )
        high = lax.ppermute(lax.slice_in_dim(block, 0, width, axis=dim), axis, backward)
        block = jnp.concatenate([low, block, high], axis=dim)
    return block


def silu_grad(pre_values):
    sigma = jax.nn.sigmoid(pre_values)
    return sigma * (1.0 + pre_values * (1.0 - sigma))


def conv_rows(padded, kernel):
    row_count = padded.shape[1] - 2
    col_count = padded.shape[2]
    channels = padded.shape[3]
    padded_cols = jnp.pad(padded, ((0, 0), (0, 0), (1, 1), (0, 0)))
    widened = jnp.concatenate(
        [padded_cols[:, :, offset : offset + col_count] for offset in range(3)], axis=3
    )
    summed = None
    for offset in range(3):
        row_block = widened[:, offset : offset + row_count].reshape(-1, 3 * channels)
        product = jnp.dot(
            row_block, kernel[offset].reshape(3 * channels, -1), preferred_element_type=jnp.float32
        )
        summed = product if summed is None else summed + product
    return summed.reshape(padded.shape[0], row_count, col_count, -1)


def group_total(values):
    return values.reshape(values.shape[0], GN_GROUPS, -1).sum(axis=2)


def spread_groups(values, channels):
    return jnp.repeat(values, channels // GN_GROUPS, axis=1)[:, None, None, :]


def cell_total(values):
    return (
        values.shape[1] * values.shape[2] * lax.axis_size("tile") * (values.shape[3] // GN_GROUPS)
    )


def moments(values):
    channels = values.shape[3]
    cell_count = cell_total(values)
    first_sum = group_total(jnp.sum(values, axis=(1, 2)))
    square_sum = group_total(jnp.sum(values * values, axis=(1, 2)))
    first_sum, square_sum = lax.psum((first_sum, square_sum), "tile")
    centre = first_sum / cell_count
    spread = square_sum / cell_count - centre * centre
    centre = spread_groups(centre, channels)
    return (centre, spread_groups(lax.rsqrt(spread + EPSILON), channels))


def with_rims(active):
    return with_halo(active, (("tile", 1),), 1)


def first_rims(active, cotangent):
    padded_first = with_rims(active)
    padded_grad = with_halo(cotangent, (("tile", 1),), 1)
    return (padded_first, padded_grad)


def norm_back_first(grad_norm, normed, inverse):
    channels = grad_norm.shape[3]
    cell_count = cell_total(grad_norm)
    plain_sum = group_total(jnp.sum(grad_norm, axis=(1, 2)))
    paired_sum = group_total(jnp.sum(grad_norm * normed, axis=(1, 2)))
    plain_sum, paired_sum = lax.psum((plain_sum, paired_sum), "tile")
    return inverse * (
        grad_norm
        - spread_groups(plain_sum / cell_count, channels)
        - normed * spread_groups(paired_sum / cell_count, channels)
    )


def body(
    images,
    cotangent,
    timesteps,
    class_ids,
    norm_gain,
    norm_bias,
    conv_first,
    conv_second,
    time_weight,
    time_bias,
    class_table,
    adaptive_weight,
    adaptive_bias,
):
    channels = images.shape[3]
    half_freq = time_weight.shape[0] // 2
    frequencies = jnp.exp(-math.log(10000.0) * jnp.arange(half_freq, dtype=jnp.float32) / half_freq)
    angles = timesteps.astype(jnp.float32)[:, None] * frequencies[None]
    sinusoid = jnp.concatenate([jnp.cos(angles), jnp.sin(angles)], axis=1)
    hidden = (
        jnp.dot(sinusoid, time_weight.astype(jnp.float32), precision=lax.Precision.HIGHEST)
        + time_bias
    )
    onehot = (class_ids[:, None] == jnp.arange(class_table.shape[0], dtype=jnp.int32)[None]).astype(
        jnp.float32
    )
    embedding = jax.nn.silu(hidden) + jnp.dot(
        onehot, class_table.astype(jnp.float32), precision=lax.Precision.HIGHEST
    )
    activated = jax.nn.silu(embedding)
    partial_terms = jnp.dot(
        activated, adaptive_weight.astype(jnp.float32), precision=lax.Precision.HIGHEST
    )
    modulation = lax.psum(partial_terms, "tile") + adaptive_bias
    factor_row = 1.0 + modulation[:, :channels]
    factor = factor_row[:, None, None, :]
    shift_term = modulation[:, channels:][:, None, None, :]
    input_float = images.astype(jnp.float32)
    centre_first, inverse_first = moments(input_float)
    normed_first = (input_float - centre_first) * inverse_first
    pre_first = normed_first * norm_gain + norm_bias
    active_first = jax.nn.silu(pre_first).astype(jnp.bfloat16)
    padded_first, padded_grad = first_rims(active_first, cotangent)
    hidden_first = conv_rows(padded_first, conv_first).astype(jnp.bfloat16)
    hidden_float = hidden_first.astype(jnp.float32)
    centre_second, inverse_second = moments(hidden_float)
    normed_second = (hidden_float - centre_second) * inverse_second
    pre_second = normed_second * factor + shift_term
    active_second = jax.nn.silu(pre_second).astype(jnp.bfloat16)
    padded_second = with_rims(active_second)
    branch = conv_rows(padded_second, conv_second).astype(jnp.bfloat16)
    flipped_second = jnp.flip(conv_second, (0, 1)).transpose(0, 1, 3, 2)
    grad_active = conv_rows(padded_grad, flipped_second)
    grad_pre = grad_active * silu_grad(pre_second)
    scale_sum = jnp.sum(grad_pre * normed_second, axis=(1, 2))
    shift_sum = jnp.sum(grad_pre, axis=(1, 2))
    scale_sum, shift_sum = lax.psum((scale_sum, shift_sum), "tile")
    cell_count = cell_total(grad_pre)
    plain_mean = group_total(shift_sum * factor_row) / cell_count
    paired_mean = group_total(scale_sum * factor_row) / cell_count
    grad_norm = grad_pre * factor
    grad_hidden = (
        inverse_second
        * (
            grad_norm
            - spread_groups(plain_mean, channels)
            - normed_second * spread_groups(paired_mean, channels)
        )
    ).astype(jnp.bfloat16)
    flipped_first = jnp.flip(conv_first, (0, 1)).transpose(0, 1, 3, 2)
    padded_hidden = with_halo(grad_hidden, (("tile", 1),), 1)
    grad_active_first = conv_rows(padded_hidden, flipped_first)
    grad_first = grad_active_first * silu_grad(pre_first) * norm_gain
    input_grad = norm_back_first(grad_first, normed_first, inverse_first).astype(jnp.bfloat16)
    pairs = jnp.concatenate([scale_sum, shift_sum], axis=1)
    local_weight = jnp.dot(activated.T, pairs, precision=lax.Precision.HIGHEST)
    local_bias = jnp.sum(pairs, axis=0)
    grad_weight, grad_bias = (
        lax.psum(local_weight.astype(jnp.bfloat16), "image").astype(jnp.float32),
        lax.psum(local_bias.astype(jnp.bfloat16), "image").astype(jnp.float32),
    )
    return (branch, input_grad, grad_weight, grad_bias)


def solution(mesh):
    return jax.shard_map(
        body,
        mesh=mesh,
        in_specs=(
            P(("groups", "image"), "tile", None, None),
            P(("groups", "image"), "tile", None, None),
            P(("groups", "image")),
            P(("groups", "image")),
            P(),
            P(),
            P(),
            P(),
            P(None, "tile"),
            P("tile"),
            P(None, "tile"),
            P("tile", None),
            P(),
        ),
        out_specs=(
            P(("groups", "image"), "tile", None, None),
            P(("groups", "image"), "tile", None, None),
            P(("groups", "tile"), None),
            P("groups"),
        ),
        check_vma=False,
    )
```

profile of v0, /device:TPU:0, one launch (start us, length us, event | category | flops | bytes accessed | tf_op | source)
XLA Modules:
  0.0 125.2 jit_solution(5303490498117019014)
XLA Ops:
  7.2 1.0 convert_reduce_fusion
  8.6 13.5 %all-reduce.7 = (f32[1,32]{1,0:T(1,128)S(1)}, f32[1,32]{1,0:T(1,128)S(1)}) all-reduce(f32[1,32]{1,0:T(1,128)S(1)} %bitcast.139, f32[1,32]{1,0:T(1,128)S(1)} %bitcast.141), channel_id=1, replica_groups=mesh['groups'=2,'tile'=4,'image'=4] {'tile'}, use_global_device_ids=true, to_apply=%region_5.6 | all-reduce | flops 64 | bytes 512 | tf_op jit(solution)/shard_map/psum | solution.py:69
  22.5 1.0 fusion.15
  23.5 0.6 fusion.55
  24.1 1.3 %collective-permute-start.1 = (bf16[1,1,64,256]{3,2,1,0:T(8,128)(2,1)}, bf16[1,1,64,256]{3,2,1,0:T(8,128)(2,1)S(1)}, u32[]{:S(2)}, u32[]{:S(2)}) collective-permute-start(bf16[1,1,64,256]{3,2,1,0:T(8,128)(2,1)} %get-tuple-element.65), channel_id=1, source_target_pairs={{4,0},{8,4},{12,8},{5,1},{9,5},{13,9},{6,2},{10,6},{14,10},{7,3},{... | collective-permute-start | bytes 98312 | tf_op jit(solution)/shard_map/ppermute | solution.py:22
  25.4 4.5 %collective-permute-start = (bf16[1,1,64,256]{3,2,1,0:T(8,128)(2,1)}, bf16[1,1,64,256]{3,2,1,0:T(8,128)(2,1)S(1)}, u32[]{:S(2)}, u32[]{:S(2)}) collective-permute-start(bf16[1,1,64,256]{3,2,1,0:T(8,128)(2,1)} %get-tuple-element.64), channel_id=1, source_target_pairs={{0,4},{4,8},{8,12},{1,5},{5,9},{9,13},{2,6},{6,10},{10,14},{3,7},{... | collective-permute-start | bytes 98312 | tf_op jit(solution)/shard_map/ppermute | solution.py:19
  30.0 1.4 %fusion.53 = (bf16[1,1,64,256]{3,2,1,0:T(8,128)(2,1)}, bf16[1,1,64,256]{3,2,1,0:T(8,128)(2,1)}) fusion(bf16[1,4,64,256]{3,2,1,0:T(8,128)(2,1)} %param.14), kind=kLoop, calls=%fused_computation.107 | loop fusion | bytes 131072 | tf_op jit(solution)/shard_map/slice | solution.py:22
  31.4 1.9 %collective-permute-start.4 = (bf16[1,1,64,256]{3,2,1,0:T(8,128)(2,1)}, bf16[1,1,64,256]{3,2,1,0:T(8,128)(2,1)S(1)}, u32[]{:S(2)}, u32[]{:S(2)}) collective-permute-start(bf16[1,1,64,256]{3,2,1,0:T(8,128)(2,1)} %get-tuple-element.61), channel_id=1, source_target_pairs={{0,4},{4,8},{8,12},{1,5},{5,9},{9,13},{2,6},{6,10},{10,14},{3,7},{... | collective-permute-start | bytes 98312 | tf_op jit(solution)/shard_map/ppermute | solution.py:19
  33.3 1.4 %collective-permute-start.5 = (bf16[1,1,64,256]{3,2,1,0:T(8,128)(2,1)}, bf16[1,1,64,256]{3,2,1,0:T(8,128)(2,1)S(1)}, u32[]{:S(2)}, u32[]{:S(2)}) collective-permute-start(bf16[1,1,64,256]{3,2,1,0:T(8,128)(2,1)} %get-tuple-element.60), channel_id=1, source_target_pairs={{4,0},{8,4},{12,8},{5,1},{9,5},{13,9},{6,2},{10,6},{14,10},{7,3},{... | collective-permute-start | bytes 98312 | tf_op jit(solution)/shard_map/ppermute | solution.py:22
  34.7 2.4 %copy.17 = bf16[3,3,256,256]{2,3,1,0:T(8,128)(2,1)} copy(bf16[3,3,256,256]{3,2,1,0:T(8,128)(2,1)} %param.20) | data formatting | bytes 2359296 | tf_op args[7]
  37.1 1.0 fusion.43
  38.1 0.6 copy-done.2
  38.7 1.0 fusion.44
  39.7 1.6 %copy.18 = bf16[3,3,256,256]{2,3,1,0:T(8,128)(2,1)} copy(bf16[3,3,256,256]{3,2,1,0:T(8,128)(2,1)S(1)} %copy-done.2) | data formatting | bytes 2359296 | tf_op args[6]
  42.8 1.0 fusion.42
  43.8 0.6 copy-done.4
  44.7 0.6 copy-done.16
  46.1 0.9 copy-done.12
  47.0 0.3 fusion.56
  47.3 0.3 convolution_add_fusion.7
  47.6 0.4 copy-done.10
  48.0 0.3 fusion.39
  48.7 11.0 %all-reduce.6 = (f32[1,512]{1,0:T(1,128)S(1)}, f32[1,32]{1,0:T(1,128)S(1)}, f32[1,32]{1,0:T(1,128)S(1)}) all-reduce(f32[1,512]{1,0:T(1,128)S(1)} %fusion.58, f32[1,32]{1,0:T(1,128)S(1)} %bitcast.134, f32[1,32]{1,0:T(1,128)S(1)} %bitcast.135), channel_id=1, replica_groups=mesh['groups'=2,'tile'=4,'image'=4] {'tile'}, use_global_device_ids=true, to_apply=%region_12.13 | all-reduce | flops 576 | bytes 4608 | tf_op jit(solution)/shard_map/psum | solution.py:133
  60.4 0.9 copy-done.8
  61.3 0.3 fusion.60
  61.6 0.3 convolution_add_fusion.3
  61.8 0.4 copy-done.13
  62.3 0.3 fusion.38
  62.6 8.5 %all-reduce.5 = (f32[1,256]{1,0:T(1,128)S(1)}, f32[1,256]{1,0:T(1,128)S(1)}) all-reduce(f32[1,256]{1,0:T(1,128)S(1)} %bitcast.136, f32[1,256]{1,0:T(1,128)S(1)} %bitcast.137), channel_id=1, replica_groups=mesh['groups'=2,'tile'=4,'image'=4] {'tile'}, use_global_device_ids=true, to_apply=%region_14.15 | all-reduce | flops 512 | bytes 4096 | tf_op jit(solution)/shard_map/psum | solution.py:156
  72.1 1.3 %collective-permute-start.3 = (bf16[1,1,64,256]{3,2,1,0:T(8,128)(2,1)S(1)}, bf16[1,1,64,256]{3,2,1,0:T(8,128)(2,1)S(1)}, u32[]{:S(2)}, u32[]{:S(2)}) collective-permute-start(bf16[1,1,64,256]{3,2,1,0:T(8,128)(2,1)S(1)} %get-tuple-element.63), channel_id=1, source_target_pairs={{4,0},{8,4},{12,8},{5,1},{9,5},{13,9},{6,2},{10,6},{14,10},{7,3},{... | collective-permute-start | bytes 98312 | tf_op jit(solution)/shard_map/ppermute | solution.py:22
  73.4 4.5 %collective-permute-start.2 = (bf16[1,1,64,256]{3,2,1,0:T(8,128)(2,1)S(1)}, bf16[1,1,64,256]{3,2,1,0:T(8,128)(2,1)S(1)}, u32[]{:S(2)}, u32[]{:S(2)}) collective-permute-start(bf16[1,1,64,256]{3,2,1,0:T(8,128)(2,1)S(1)} %get-tuple-element.62), channel_id=1, source_target_pairs={{0,4},{4,8},{8,12},{1,5},{5,9},{9,13},{2,6},{6,10},{10,14},{3,7},{... | collective-permute-start | bytes 98312 | tf_op jit(solution)/shard_map/ppermute | solution.py:19
  77.9 0.8 multiply_convert_fusion
  78.8 1.3 %collective-permute-start.7 = (bf16[1,1,64,256]{3,2,1,0:T(8,128)(2,1)S(1)}, bf16[1,1,64,256]{3,2,1,0:T(8,128)(2,1)S(1)}, u32[]{:S(2)}, u32[]{:S(2)}) collective-permute-start(bf16[1,1,64,256]{3,2,1,0:T(8,128)(2,1)S(1)} %get-tuple-element.59), channel_id=1, source_target_pairs={{4,0},{8,4},{12,8},{5,1},{9,5},{13,9},{6,2},{10,6},{14,10},{7,3},{... | collective-permute-start | bytes 98312 | tf_op jit(solution)/shard_map/ppermute | solution.py:22
  80.1 4.5 %collective-permute-start.6 = (bf16[1,1,64,256]{3,2,1,0:T(8,128)(2,1)S(1)}, bf16[1,1,64,256]{3,2,1,0:T(8,128)(2,1)S(1)}, u32[]{:S(2)}, u32[]{:S(2)}) collective-permute-start(bf16[1,1,64,256]{3,2,1,0:T(8,128)(2,1)S(1)} %get-tuple-element.58), channel_id=1, source_target_pairs={{0,4},{4,8},{8,12},{1,5},{5,9},{9,13},{2,6},{6,10},{10,14},{3,7},{... | collective-permute-start | bytes 98312 | tf_op jit(solution)/shard_map/ppermute | solution.py:19
  84.6 5.7 %psum.87 = bf16[512]{0:T(512)(128)(2,1)S(1)} all-reduce(bf16[512]{0:T(512)(128)(2,1)S(1)} %convert_element_type.135), channel_id=1, replica_groups=mesh['groups'=2,'tile'=4,'image'=4] {'image'}, use_global_device_ids=true, to_apply=%region_26.27 | all-reduce | flops 512 | bytes 2048 | tf_op jit(solution)/shard_map/psum | solution.py:179
  90.3 0.6 convert_element_type.136
  91.1 0.9 fusion.47
  92.2 0.3 fusion.61
  92.6 0.3 convolution_add_fusion.1
  92.9 0.3 convolution_add_fusion
  93.1 0.3 copy-done.5
  94.0 10.2 %all-reduce.4 = (f32[1,32]{1,0:T(1,128)S(1)}, f32[1,32]{1,0:T(1,128)S(1)}) all-reduce(f32[1,32]{1,0:T(1,128)S(1)} %bitcast.138, f32[1,32]{1,0:T(1,128)S(1)} %bitcast.140), channel_id=1, replica_groups=mesh['groups'=2,'tile'=4,'image'=4] {'tile'}, use_global_device_ids=true, to_apply=%region_24.25 | all-reduce | flops 64 | bytes 512 | tf_op jit(solution)/shard_map/psum | solution.py:91
  104.6 0.3 fusion.59
  104.9 0.3 convolution_add_fusion.5
  105.2 0.9 fusion.2
  106.1 0.7 fusion.23
  106.9 9.7 %all-reduce.10.cloned.1.call-done = bf16[256,512]{1,0:T(8,128)(2,1)} async-done(((bf16[256,512]{1,0:T(8,128)(2,1)}), bf16[256,512]{1,0:T(8,128)(2,1)}) %all-reduce.10.cloned.1.call-update) | async-done | bytes 262160 | tf_op jit(solution)/shard_map/psum | solution.py:178
  116.6 1.8 %convert_element_type.134 = f32[256,512]{1,0:T(8,128)} convert(bf16[256,512]{1,0:T(8,128)(2,1)} %all-reduce.10.cloned.1.call-done) | non-fusion elementwise | flops 131072 | bytes 786432 | tf_op jit(solution)/shard_map/convert_element_type | solution.py:178
  (118 shorter events, 5.4 us)
Async XLA Ops:
  7.2 37.4 %copy-start = (bf16[1000,256]{1,0:T(8,128)(2,1)S(1)}, bf16[1000,256]{1,0:T(8,128)(2,1)}, u32[]{:S(2)}) copy-start(bf16[1000,256]{1,0:T(8,128)(2,1)} %param.23) | copy-start | bytes 1536004
  7.2 109.4 %all-reduce.10.cloned.1.call-start = ((), (), s32[]{:S(2)}) async-start(), calls=%async_computation | async-start | bytes 524288 | tf_op jit(solution)/shard_map/psum | solution.py:178
  24.1 21.6 %collective-permute-start.1 = (bf16[1,1,64,256]{3,2,1,0:T(8,128)(2,1)}, bf16[1,1,64,256]{3,2,1,0:T(8,128)(2,1)S(1)}, u32[]{:S(2)}, u32[]{:S(2)}) collective-permute-start(bf16[1,1,64,256]{3,2,1,0:T(8,128)(2,1)} %get-tuple-element.65), channel_id=1, source_target_pairs={{4,0},{8,4},{12,8},{5,1},{9,5},{13,9},{6,2},{10,6},{14,10},{7,3},{... | collective-permute-start | bytes 98312 | tf_op jit(solution)/shard_map/ppermute | solution.py:22
  25.4 20.4 %collective-permute-start = (bf16[1,1,64,256]{3,2,1,0:T(8,128)(2,1)}, bf16[1,1,64,256]{3,2,1,0:T(8,128)(2,1)S(1)}, u32[]{:S(2)}, u32[]{:S(2)}) collective-permute-start(bf16[1,1,64,256]{3,2,1,0:T(8,128)(2,1)} %get-tuple-element.64), channel_id=1, source_target_pairs={{0,4},{4,8},{8,12},{1,5},{5,9},{9,13},{2,6},{6,10},{10,14},{3,7},{... | collective-permute-start | bytes 98312 | tf_op jit(solution)/shard_map/ppermute | solution.py:19
  31.4 28.4 %collective-permute-start.4 = (bf16[1,1,64,256]{3,2,1,0:T(8,128)(2,1)}, bf16[1,1,64,256]{3,2,1,0:T(8,128)(2,1)S(1)}, u32[]{:S(2)}, u32[]{:S(2)}) collective-permute-start(bf16[1,1,64,256]{3,2,1,0:T(8,128)(2,1)} %get-tuple-element.61), channel_id=1, source_target_pairs={{0,4},{4,8},{8,12},{1,5},{5,9},{9,13},{2,6},{6,10},{10,14},{3,7},{... | collective-permute-start | bytes 98312 | tf_op jit(solution)/shard_map/ppermute | solution.py:19
  33.3 3.8 %copy-start.1 = (bf16[3,3,256,256]{3,2,1,0:T(8,128)(2,1)S(1)}, bf16[3,3,256,256]{3,2,1,0:T(8,128)(2,1)}, u32[]{:S(2)}) copy-start(bf16[3,3,256,256]{3,2,1,0:T(8,128)(2,1)} %param.20) | copy-start | bytes 3538948
  33.3 26.8 %collective-permute-start.5 = (bf16[1,1,64,256]{3,2,1,0:T(8,128)(2,1)}, bf16[1,1,64,256]{3,2,1,0:T(8,128)(2,1)S(1)}, u32[]{:S(2)}, u32[]{:S(2)}) collective-permute-start(bf16[1,1,64,256]{3,2,1,0:T(8,128)(2,1)} %get-tuple-element.60), channel_id=1, source_target_pairs={{4,0},{8,4},{12,8},{5,1},{9,5},{13,9},{6,2},{10,6},{14,10},{7,3},{... | collective-permute-start | bytes 98312 | tf_op jit(solution)/shard_map/ppermute | solution.py:22
  37.1 1.6 %copy-start.2 = (bf16[3,3,256,256]{3,2,1,0:T(8,128)(2,1)S(1)}, bf16[3,3,256,256]{3,2,1,0:T(8,128)(2,1)}, u32[]{:S(2)}) copy-start(bf16[3,3,256,256]{3,2,1,0:T(8,128)(2,1)} %param.19) | copy-start | bytes 3538948
  39.7 3.0 %copy-start.3 = (bf16[3,3,256,256]{2,3,1,0:T(8,128)(2,1)S(1)}, bf16[3,3,256,256]{2,3,1,0:T(8,128)(2,1)}, u32[]{:S(2)}) copy-start(bf16[3,3,256,256]{2,3,1,0:T(8,128)(2,1)} %copy.17) | copy-start | bytes 3538948
  42.8 1.6 %copy-start.4 = (bf16[3,3,256,256]{2,3,1,0:T(8,128)(2,1)S(1)}, bf16[3,3,256,256]{2,3,1,0:T(8,128)(2,1)}, u32[]{:S(2)}) copy-start(bf16[3,3,256,256]{2,3,1,0:T(8,128)(2,1)} %copy.18) | copy-start | bytes 3538948
  44.4 0.9 copy-start.16
  44.4 1.0 copy-start.20
  44.5 1.1 copy-start.15
  46.0 1.0 copy-start.12
  46.0 1.3 %copy-start.11 = (bf16[1,3,256,256]{3,2,1,0:T(8,128)(2,1)S(1)}, bf16[1,3,256,256]{3,2,1,0:T(8,128)(2,1)}, u32[]{:S(2)}) copy-start(bf16[1,3,256,256]{3,2,1,0:T(8,128)(2,1)} %get-tuple-element.34) | copy-start | bytes 1179652
  47.0 1.0 copy-start.10
  47.3 12.5 %copy-start.19 = (f32[512]{0:T(512)S(1)}, f32[512]{0:T(512)}, u32[]{:S(2)}) copy-start(f32[512]{0:T(512)} %param.25) | copy-start | bytes 6148
  47.3 12.5 %copy-start.14 = (bf16[1,4,64,256]{3,2,1,0:T(8,128)(2,1)S(1)}, bf16[1,4,64,256]{3,2,1,0:T(8,128)(2,1)}, u32[]{:S(2)}) copy-start(bf16[1,4,64,256]{3,2,1,0:T(8,128)(2,1)} %param.14) | copy-start | bytes 393220
  60.3 1.0 copy-start.8
  61.3 1.0 copy-start.13
  72.1 18.8 %collective-permute-start.3 = (bf16[1,1,64,256]{3,2,1,0:T(8,128)(2,1)S(1)}, bf16[1,1,64,256]{3,2,1,0:T(8,128)(2,1)S(1)}, u32[]{:S(2)}, u32[]{:S(2)}) collective-permute-start(bf16[1,1,64,256]{3,2,1,0:T(8,128)(2,1)S(1)} %get-tuple-element.63), channel_id=1, source_target_pairs={{4,0},{8,4},{12,8},{5,1},{9,5},{13,9},{6,2},{10,6},{14,10},{7,3},{... | collective-permute-start | bytes 98312 | tf_op jit(solution)/shard_map/ppermute | solution.py:22
  73.4 17.5 %collective-permute-start.2 = (bf16[1,1,64,256]{3,2,1,0:T(8,128)(2,1)S(1)}, bf16[1,1,64,256]{3,2,1,0:T(8,128)(2,1)S(1)}, u32[]{:S(2)}, u32[]{:S(2)}) collective-permute-start(bf16[1,1,64,256]{3,2,1,0:T(8,128)(2,1)S(1)} %get-tuple-element.62), channel_id=1, source_target_pairs={{0,4},{4,8},{8,12},{1,5},{5,9},{9,13},{2,6},{6,10},{10,14},{3,7},{... | collective-permute-start | bytes 98312 | tf_op jit(solution)/shard_map/ppermute | solution.py:19
  78.8 13.2 %collective-permute-start.7 = (bf16[1,1,64,256]{3,2,1,0:T(8,128)(2,1)S(1)}, bf16[1,1,64,256]{3,2,1,0:T(8,128)(2,1)S(1)}, u32[]{:S(2)}, u32[]{:S(2)}) collective-permute-start(bf16[1,1,64,256]{3,2,1,0:T(8,128)(2,1)S(1)} %get-tuple-element.59), channel_id=1, source_target_pairs={{4,0},{8,4},{12,8},{5,1},{9,5},{13,9},{6,2},{10,6},{14,10},{7,3},{... | collective-permute-start | bytes 98312 | tf_op jit(solution)/shard_map/ppermute | solution.py:22
  80.1 11.9 %collective-permute-start.6 = (bf16[1,1,64,256]{3,2,1,0:T(8,128)(2,1)S(1)}, bf16[1,1,64,256]{3,2,1,0:T(8,128)(2,1)S(1)}, u32[]{:S(2)}, u32[]{:S(2)}) collective-permute-start(bf16[1,1,64,256]{3,2,1,0:T(8,128)(2,1)S(1)} %get-tuple-element.58), channel_id=1, source_target_pairs={{0,4},{4,8},{8,12},{1,5},{5,9},{9,13},{2,6},{6,10},{10,14},{3,7},{... | collective-permute-start | bytes 98312 | tf_op jit(solution)/shard_map/ppermute | solution.py:19
  92.5 0.9 copy-start.5
  92.5 0.9 copy-start.17
  92.5 0.9 copy-start.18
  92.8 11.8 %copy-start.7 = (bf16[1,3,256,256]{3,2,1,0:T(8,128)(2,1)S(1)}, bf16[1,3,256,256]{3,2,1,0:T(8,128)(2,1)}, u32[]{:S(2)}) copy-start(bf16[1,3,256,256]{3,2,1,0:T(8,128)(2,1)} %get-tuple-element.32) | copy-start | bytes 1179652
  92.8 11.8 %copy-start.9 = (bf16[1,4,64,768]{3,2,1,0:T(8,128)(2,1)S(1)}, bf16[1,4,64,768]{3,2,1,0:T(8,128)(2,1)}, u32[]{:S(2)}) copy-start(bf16[1,4,64,768]{3,2,1,0:T(8,128)(2,1)} %get-tuple-element.44) | copy-start | bytes 1179652
  93.4 11.5 %copy-start.6 = (bf16[1,3,256,256]{3,2,1,0:T(8,128)(2,1)S(1)}, bf16[1,3,256,256]{3,2,1,0:T(8,128)(2,1)}, u32[]{:S(2)}) copy-start(bf16[1,3,256,256]{3,2,1,0:T(8,128)(2,1)} %get-tuple-element.31) | copy-start | bytes 1179652
Sparse Core Ops, SparseCore 0:
  84.8 31.7 all-reduce.9
where the time goes:
time: 126 us; the launch traced here: 125 us
  blocking collectives  48.9 us (39%)
  starting transfers between devices  20.9 us (17%)
  local copies, waits for them, and re-layouts  17.4 us (14%)
  between operations  16 us (13%)
  waiting for transfers between devices  9.77 us (8%)
  other arithmetic  7.85 us (6%)
  matrix products  4.46 us (4%)
    ppermute x4, starting transfers between devices, with_halo(): lax.ppermute(lax.slice_in_dim(block, block.shape[dim] - width, None, axis...  15.6 us
    psum x1, blocking collectives, moments(): first_sum, square_sum = lax.psum((first_sum, square_sum), 'tile')  13.5 us
    psum x1, blocking collectives, body(): modulation = lax.psum(partial_terms, 'tile') + adaptive_bias  11 us
    psum x1, blocking collectives, norm_back_first(): plain_sum, paired_sum = lax.psum((plain_sum, paired_sum), 'tile')  10.2 us
    psum x1, waiting for transfers between devices, body(): lax.psum(local_weight.astype(jnp.bfloat16), 'image').astype(jnp.float32)  9.73 us
    unnamed x46, local copies, waits for them, and re-layouts  8.78 us
    psum x1, blocking collectives, body(): scale_sum, shift_sum = lax.psum((scale_sum, shift_sum), 'tile')  8.47 us
    psum x1, blocking collectives, body(): lax.psum(local_bias.astype(jnp.bfloat16), 'image').astype(jnp.float32)  5.67 us
  transfers between devices with their start and end apart: 9, of which 1 were waited for; matrix products, arithmetic and copies ran while one was open for 14% of the time, Pallas kernels for 0%

commit v1 on v0

v1 whole, which is shorter than its diff:
```python
import functools
import math

import jax
import jax.numpy as jnp
from jax import lax
from jax.experimental import pallas as pl
from jax.experimental.pallas import tpu as pltpu
from jax.sharding import PartitionSpec as P

GN_GROUPS = 32
EPSILON = 1e-05
MESH = pl.DeviceIdType.MESH
F32 = jnp.float32
BF16 = jnp.bfloat16
REACH = 2
HIGHEST = lax.Precision.HIGHEST


def group_spread(values, width):
    count = values.shape[-1]
    lane = lax.broadcasted_iota(jnp.int32, values.shape, values.ndim - 1)
    step = 1
    while step < width:
        up = pltpu.roll(values, step, values.ndim - 1)
        down = pltpu.roll(values, count - step, values.ndim - 1)
        values = values + jnp.where((lane & step) != 0, up, down)
        step *= 2
    return values


def silu_slope(pre, sigma):
    return sigma * (1.0 + pre * (1.0 - sigma))


def column_sums(first, second):
    return jnp.concatenate(
        [jnp.sum(first, axis=0, keepdims=True), jnp.sum(second, axis=0, keepdims=True)], axis=0
    )


def kernel(
    n, m,
    steps_ref, ids_ref, gain_ref, bias_ref, tbias_ref, abias_ref,
    images_hbm, cot_hbm, first_hbm, second_hbm, tweight_hbm, table_hbm, aweight_hbm,
    branch_hbm, igrad_hbm, wgrad_hbm, bgrad_ref,
    images, cot, first, second, tweight, table, aweight,
    wide_first, wide_cot, wide_second, wide_hidden,
    hidden, gact, nsecond, gpre, nfirst, slope, branch, igrad, wgrad,
    slots, acts, pairs,
    load_sem, store_sem, halo_send, halo_recv, send_sem, recv_sem,
    act_send, act_recv, pair_send, pair_recv,
):
    me = lax.axis_index("tile")
    mine = lax.axis_index("image")
    rows, cols, channels = images_hbm.shape[1:]
    width = channels // GN_GROUPS
    cells = float(rows * cols * n * width)
    own = rows * cols
    rim = cols
    above, below = me > 0, me < n - 1

    loads = [
        pltpu.make_async_copy(source, target, load_sem.at[k])
        for k, (source, target) in enumerate(
            [
                (images_hbm.at[0], images.at[pl.ds(REACH, rows)]),
                (cot_hbm.at[0], cot.at[pl.ds(REACH, rows)]),
                (tweight_hbm, tweight),
                (table_hbm, table),
                (aweight_hbm, aweight),
                (first_hbm, first),
                (second_hbm, second),
            ]
        )
    ]
    for load in loads:
        load.start()

    barrier = pltpu.get_barrier_semaphore()
    for k in range(1, n):
        pl.semaphore_signal(
            barrier, inc=1, device_id={"tile": lax.rem(me + k, n)}, device_id_type=MESH
        )
    for k in range(1, m):
        pl.semaphore_signal(
            barrier, inc=1, device_id={"image": lax.rem(mine + k, m)}, device_id_type=MESH
        )

    def tile_copy(stage, k, arriving):
        peer = lax.rem(me + k, n)
        slot = lax.rem(me + n - k, n) if arriving else me
        return pltpu.make_async_remote_copy(
            src_ref=slots.at[stage, slot],
            dst_ref=slots.at[stage, slot],
            send_sem=send_sem.at[stage, k],
            recv_sem=recv_sem.at[stage, k],
            device_id={"tile": peer},
            device_id_type=MESH,
        )

    def share(stage, value):
        slots[stage, me] = value
        for k in range(1, n):
            tile_copy(stage, k, False).start()

    def total(stage):
        for k in range(1, n):
            tile_copy(stage, k, True).wait_recv()
        summed = slots[stage, 0]
        for k in range(1, n):
            summed = summed + slots[stage, k]
        return summed

    def image_copy(buffer, sends, receives, k, arriving):
        peer = lax.rem(mine + k, m)
        slot = lax.rem(mine + m - k, m) if arriving else mine
        return pltpu.make_async_remote_copy(
            src_ref=buffer.at[slot],
            dst_ref=buffer.at[slot],
            send_sem=sends.at[k],
            recv_sem=receives.at[k],
            device_id={"image": peer},
            device_id_type=MESH,
        )

    def halo_copy(which, buffer, up):
        source = pl.ds(REACH, REACH) if up else pl.ds(rows, REACH)
        target = pl.ds(rows + REACH, REACH) if up else pl.ds(0, REACH)
        return pltpu.make_async_remote_copy(
            src_ref=buffer.at[source],
            dst_ref=buffer.at[target],
            send_sem=halo_send.at[which, int(up)],
            recv_sem=halo_recv.at[which, int(up)],
            device_id={"tile": me - 1 if up else me + 1},
            device_id_type=MESH,
        )

    def flat(buffer, start, count):
        return buffer[pl.ds(start, count)].reshape(count * cols, channels).astype(F32)

    def widen(wide, start, values):
        count = values.shape[0]
        column = lax.rem(lax.broadcasted_iota(jnp.int32, values.shape, 0), cols)
        before = jnp.where(column == 0, 0.0, pltpu.roll(values, 1, 0))
        after = jnp.where(column == cols - 1, 0.0, pltpu.roll(values, count - 1, 0))
        at = pl.ds(start * cols, count)
        wide[at, 0:channels] = before.astype(BF16)
        wide[at, channels : 2 * channels] = values.astype(BF16)
        wide[at, 2 * channels : 3 * channels] = after.astype(BF16)

    def conv(wide, start, count, weight):
        summed = None
        for i in range(3):
            product = jnp.dot(
                wide[pl.ds((start + i) * cols, count * cols), :],
                weight[i].reshape(3 * channels, channels),
                preferred_element_type=F32,
            )
            summed = product if summed is None else summed + product
        return summed

    def conv_back(wide, start, count, weight):
        summed = None
        for i in range(3):
            for j in range(3):
                product = lax.dot_general(
                    wide[pl.ds((start + i) * cols, count * cols), j * channels : (j + 1) * channels],
                    weight[2 - i, 2 - j],
                    (((1,), (1,)), ((), ())),
                    preferred_element_type=F32,
                )
                summed = product if summed is None else summed + product
        return summed

    def moments(summed):
        spread = group_spread(summed, width) / cells
        centre = spread[0:1]
        variance = jnp.maximum(spread[1:2] - centre * centre, 0.0)
        return centre, lax.rsqrt(variance + EPSILON)

    loads[0].wait()
    values = flat(images, REACH, rows)
    sums = column_sums(values, values * values)
    loads[1].wait()
    pl.semaphore_wait(barrier, n - 1 + m - 1)
    share(0, sums)
    for which, buffer in enumerate((images, cot)):

        @pl.when(above)
        def _():
            halo_copy(which, buffer, True).start()

        @pl.when(below)
        def _():
            halo_copy(which, buffer, False).start()

        @pl.when(jnp.logical_not(above))
        def _():
            buffer[pl.ds(0, REACH)] = jnp.zeros((REACH, cols, channels), BF16)

        @pl.when(jnp.logical_not(below))
        def _():
            buffer[pl.ds(rows + REACH, REACH)] = jnp.zeros((REACH, cols, channels), BF16)

    for k in (2, 3, 4):
        loads[k].wait()
    half = tweight.shape[0] // 2
    index = lax.broadcasted_iota(jnp.int32, (half, 1), 0).astype(F32)
    angles = steps_ref[0].astype(F32) * jnp.exp(-math.log(10000.0) * index / half)
    pre_time = (
        jnp.sum(jnp.cos(angles) * tweight[0:half].astype(F32), axis=0, keepdims=True)
        + jnp.sum(jnp.sin(angles) * tweight[half:].astype(F32), axis=0, keepdims=True)
        + tbias_ref[...]
    )
    entry = lax.broadcasted_iota(jnp.int32, table.shape, 0) == ids_ref[0]
    picked = jnp.sum(jnp.where(entry, table[...].astype(F32), 0.0), axis=0, keepdims=True)
    embedding = pre_time * jax.nn.sigmoid(pre_time) + picked
    activated = embedding * jax.nn.sigmoid(embedding)
    acts[mine] = activated
    for k in range(1, m):
        image_copy(acts, act_send, act_recv, k, False).start()
    partial = jnp.dot(
        jnp.broadcast_to(activated, (8, activated.shape[1])),
        aweight[...].astype(F32),
        precision=HIGHEST,
        preferred_element_type=F32,
    )[0:1]
    share(1, jnp.concatenate([partial[:, :channels], partial[:, channels:]], axis=0))

    gain, bias = gain_ref[...], bias_ref[...]
    centre, inverse_first = moments(total(0))

    def first_activation(normed):
        pre = normed * gain + bias
        return pre, jax.nn.sigmoid(pre)

    values = (flat(images, REACH, rows) - centre) * inverse_first
    pre, sigma = first_activation(values)
    widen(wide_first, REACH, pre * sigma)

    def halo_wait(which, buffer):
        @pl.when(below)
        def _():
            halo_copy(which, buffer, True).wait_recv()

        @pl.when(above)
        def _():
            halo_copy(which, buffer, False).wait_recv()

    halo_wait(0, images)
    for start, inside in ((0, above), (rows + REACH, below)):
        rim_values = (flat(images, start, REACH) - centre) * inverse_first
        rim_pre, rim_sigma = first_activation(rim_values)
        widen(wide_first, start, jnp.where(inside, rim_pre * rim_sigma, 0.0))
    loads[5].wait()
    centre_rows = conv(wide_first, 1, rows, first).astype(BF16).astype(F32)
    share(2, column_sums(centre_rows, centre_rows * centre_rows))
    hidden[pl.ds(rim, own)] = centre_rows

    for row in (0, rows + 1):
        hidden[pl.ds(row * cols, cols)] = conv(wide_first, row, 1, first).astype(BF16).astype(F32)
    halo_wait(1, cot)
    widen(wide_cot, 0, flat(cot, 0, rows + 2 * REACH))
    loads[6].wait()
    gact[...] = conv_back(wide_cot, 0, rows + 2, second)
    values = (flat(images, REACH, rows) - centre) * inverse_first
    pre, sigma = first_activation(values)
    nfirst[...] = values
    slope[...] = silu_slope(pre, sigma) * gain

    modulation = total(1)
    factor = 1.0 + (modulation[0:1] + abias_ref[:, :channels])
    shift = modulation[1:2] + abias_ref[:, channels:]
    centre, inverse_second = moments(total(2))
    for start, count, inside in ((1, rows, None), (0, 1, above), (rows + 1, 1, below)):
        at = pl.ds(start * cols, count * cols)
        normed = (hidden[at] - centre) * inverse_second
        pre = normed * factor + shift
        sigma = jax.nn.sigmoid(pre)
        back = gact[at] * silu_slope(pre, sigma)
        if inside is None:
            share(3, column_sums(back * normed, back))
        active = pre * sigma
        if inside is not None:
            active = jnp.where(inside, active, 0.0)
        widen(wide_second, start, active)
        nsecond[at] = normed
        gpre[at] = back

    branch[...] = conv(wide_second, 0, rows, second).astype(BF16).reshape(rows, cols, channels)
    stores = [pltpu.make_async_copy(branch, branch_hbm.at[0], store_sem.at[0])]
    stores[0].start()

    sums = total(3)
    spread = group_spread(sums * factor, width) / cells
    paired_mean, plain_mean = spread[0:1], spread[1:2]
    for start, count, inside in ((1, rows, None), (0, 1, above), (rows + 1, 1, below)):
        at = pl.ds(start * cols, count * cols)
        back = inverse_second * (gpre[at] * factor - plain_mean - nsecond[at] * paired_mean)
        if inside is not None:
            back = jnp.where(inside, back, 0.0)
        widen(wide_hidden, start, back)
    pairs[mine] = sums
    for k in range(1, m):
        image_copy(pairs, pair_send, pair_recv, k, False).start()
    back = conv_back(wide_hidden, 0, rows, first) * slope[...]
    normed = nfirst[...]
    share(4, column_sums(back, back * normed))

    for k in range(1, m):
        image_copy(acts, act_send, act_recv, k, True).wait_recv()
        image_copy(pairs, pair_send, pair_recv, k, True).wait_recv()
    extra = (-m) % 8

    def stacked(pieces):
        if extra:
            pieces = pieces + [jnp.zeros((extra, pieces[0].shape[1]), F32)]
        return jnp.concatenate(pieces, axis=0)

    left = stacked([acts[k] for k in range(m)])
    for part in range(2):
        right = stacked([pairs[k][part : part + 1] for k in range(m)])
        columns = slice(part * channels, (part + 1) * channels)
        wgrad[:, columns] = lax.dot_general(
            left, right, (((0,), (0,)), ((), ())), precision=HIGHEST, preferred_element_type=F32
        )
        bgrad_ref[:, columns] = jnp.sum(right, axis=0, keepdims=True)
    stores.append(pltpu.make_async_copy(wgrad, wgrad_hbm, store_sem.at[1]))
    stores[1].start()

    spread = group_spread(total(4), width) / cells
    result = inverse_first * (back - spread[0:1] - normed * spread[1:2])
    igrad[...] = result.astype(BF16).reshape(rows, cols, channels)
    stores.append(pltpu.make_async_copy(igrad, igrad_hbm.at[0], store_sem.at[2]))
    stores[2].start()

    for stage in range(5):
        for k in range(1, n):
            tile_copy(stage, k, False).wait_send()
    for k in range(1, m):
        image_copy(acts, act_send, act_recv, k, False).wait_send()
        image_copy(pairs, pair_send, pair_recv, k, False).wait_send()
    for which, buffer in enumerate((images, cot)):

        @pl.when(above)
        def _():
            halo_copy(which, buffer, True).wait_send()

        @pl.when(below)
        def _():
            halo_copy(which, buffer, False).wait_send()

    for store in stores:
        store.wait()


def body(
    n, m,
    images, cotangent, timesteps, class_ids, norm_gain, norm_bias, conv_first, conv_second,
    time_weight, time_bias, class_table, adaptive_weight, adaptive_bias,
):
    count, rows, cols, channels = images.shape
    assert count == 1 and rows >= REACH
    emb = time_weight.shape[1]
    smem = pl.BlockSpec(memory_space=pltpu.SMEM)
    vmem = pl.BlockSpec(memory_space=pltpu.VMEM)
    anywhere = pl.BlockSpec(memory_space=pl.ANY)
    padded = rows + 2 * REACH
    own, more, most = rows * cols, (rows + 2) * cols, padded * cols
    dma = pltpu.SemaphoreType.DMA
    branch, igrad, wgrad, bgrad = pl.pallas_call(
        functools.partial(kernel, n, m),
        out_shape=(
            jax.ShapeDtypeStruct(images.shape, BF16),
            jax.ShapeDtypeStruct(images.shape, BF16),
            jax.ShapeDtypeStruct((emb, 2 * channels), F32),
            jax.ShapeDtypeStruct((1, 2 * channels), F32),
        ),
        in_specs=[smem] * 2 + [vmem] * 4 + [anywhere] * 7,
        out_specs=(anywhere, anywhere, anywhere, vmem),
        scratch_shapes=[
            pltpu.VMEM((padded, cols, channels), BF16),
            pltpu.VMEM((padded, cols, channels), BF16),
            pltpu.VMEM(conv_first.shape, BF16),
            pltpu.VMEM(conv_second.shape, BF16),
            pltpu.VMEM(time_weight.shape, BF16),
            pltpu.VMEM(class_table.shape, BF16),
            pltpu.VMEM(adaptive_weight.shape, BF16),
            pltpu.VMEM((most, 3 * channels), BF16),
            pltpu.VMEM((most, 3 * channels), BF16),
            pltpu.VMEM((more, 3 * channels), BF16),
            pltpu.VMEM((more, 3 * channels), BF16),
            pltpu.VMEM((more, channels), F32),
            pltpu.VMEM((more, channels), F32),
            pltpu.VMEM((more, channels), F32),
            pltpu.VMEM((more, channels), F32),
            pltpu.VMEM((own, channels), F32),
            pltpu.VMEM((own, channels), F32),
            pltpu.VMEM((rows, cols, channels), BF16),
            pltpu.VMEM((rows, cols, channels), BF16),
            pltpu.VMEM((emb, 2 * channels), F32),
            pltpu.VMEM((5, n, 2, channels), F32),
            pltpu.VMEM((m, 1, emb), F32),
            pltpu.VMEM((m, 2, channels), F32),
            dma((7,)),
            dma((3,)),
            dma((2, 2)),
            dma((2, 2)),
            dma((5, n)),
            dma((5, n)),
            dma((m,)),
            dma((m,)),
            dma((m,)),
            dma((m,)),
        ],
        compiler_params=pltpu.CompilerParams(collective_id=0, has_side_effects=True),
    )(
        timesteps, class_ids, norm_gain[None], norm_bias[None], time_bias[None],
        adaptive_bias[None], images, cotangent, conv_first, conv_second, time_weight,
        class_table, adaptive_weight,
    )
    return branch, igrad, wgrad, bgrad[0]


def solution(mesh):
    return jax.shard_map(
        functools.partial(body, mesh.shape["tile"], mesh.shape["image"]),
        mesh=mesh,
        in_specs=(
            P(("groups", "image"), "tile", None, None),
            P(("groups", "image"), "tile", None, None),
            P(("groups", "image")),
            P(("groups", "image")),
            P(),
            P(),
            P(),
            P(),
            P(None, "tile"),
            P("tile"),
            P(None, "tile"),
            P("tile", None),
            P(),
        ),
        out_specs=(
            P(("groups", "image"), "tile", None, None),
            P(("groups", "image"), "tile", None, None),
            P(("groups", "tile"), None),
            P("groups"),
        ),
        check_vma=False,
    )
```

time: 126 us -> 32.5 us (0.26)
  blocking collectives: 48.9 us -> 0 us
  Pallas kernels: 0 us -> 24.7 us
  starting transfers between devices: 20.9 us -> 0 us
  between operations: 16 us -> 1.94 us
  local copies, waits for them, and re-layouts: 17.4 us -> 5.59 us
  waiting for transfers between devices: 9.77 us -> 0 us
  other arithmetic: 7.85 us -> 0 us
  matrix products: 4.46 us -> 0 us
    psum x5 -> x0, blocking collectives: 48.9 us -> none  [the longest x1 13.5 us: moments(): first_sum, square_sum = lax.psum((first_sum, square_sum), 'tile')]
    pallas_call x0 -> x1, Pallas kernels: none -> 24.7 us  [body(): pl.pallas_call(functools.partial(kernel, n, m), out_shape=(jax.ShapeDtype...]
    ppermute x8 -> x0, starting transfers between devices: 20.8 us -> none  [the longest x4 15.6 us: with_halo(): lax.ppermute(lax.slice_in_dim(block, block.shape[dim] - width, None, axis...]
    psum x1 -> x0, waiting for transfers between devices: 9.73 us -> none  [body(): lax.psum(local_weight.astype(jnp.bfloat16), 'image').astype(jnp.float32)]
    slice x16 -> x0, local copies, waits for them, and re-layouts: 6.5 us -> none  [the longest x4 3.03 us: conv_rows(): kernel[offset].reshape(3 * channels, -1)]
    convert_element_type x7 -> x0, other arithmetic: 5.14 us -> none  [the longest x1 1.8 us: body(): lax.psum(local_weight.astype(jnp.bfloat16), 'image').astype(jnp.float32)]
    dot_general x15 -> x0, matrix products: 4.46 us -> none  [the longest x12 3.94 us: conv_rows(): jnp.dot(row_block, kernel[offset].reshape(3 * channels, -1), preferred_el...]
    unnamed x46 -> x6, local copies, waits for them, and re-layouts: 8.78 us -> 5.59 us
  transfers between devices with their start and end apart: 9 -> 0, of which waited for: 1 -> 0; matrix products, arithmetic and copies ran while one was open for 14% -> 0% of each run, Pallas kernels for 0% -> 0%
where the time goes in v1:
time: 32.5 us; the launch traced here: 32.3 us
  Pallas kernels  24.7 us (76%)
  local copies, waits for them, and re-layouts  5.59 us (17%)
  between operations  1.94 us (6%)
    pallas_call x1, Pallas kernels, body(): pl.pallas_call(functools.partial(kernel, n, m), out_shape=(jax.ShapeDtype...  24.7 us
    unnamed x6, local copies, waits for them, and re-layouts  5.59 us

profile of v1, /device:TPU:0, one launch (start us, length us, event | category | flops | bytes accessed | tf_op | source)
XLA Modules:
  0.0 32.3 jit_solution(6775982318334719522)
XLA Ops:
  1.9 24.7 %shard_map.156 = (bf16[1,4,64,256]{3,2,1,0:T(8,128)(2,1)}, bf16[1,4,64,256]{3,2,1,0:T(8,128)(2,1)}, f32[256,512]{1,0:T(8,128)}, f32[1,512]{1,0:T(1,128)}) custom-call(s32[1]{0:T(128)S(6)} %copy.21.steps_ref, s32[1]{0:T(128)S(6)} %copy.22.ids_ref, f32[1,256]{1,0:T(1,128)} %bitcast.7, f32[1,256]{1,0:T(1,128)} %bitcast.8, f32[1,256]{1,0:T(1,128)} %bitcast.9, ...), custom_call_target="tpu_custom_call" | custom-call | tf_op jit(solution)/shard_map/pallas_call | solution.py:372
  26.7 0.0 copy-start
  26.7 1.6 %copy.23 = bf16[1,4,64,256]{3,2,1,0:T(8,128)(2,1)} copy(bf16[1,4,64,256]{3,2,1,0:T(8,128)(2,1)} %get-tuple-element.16) | data formatting | bytes 262144
  28.3 1.6 %copy.24 = bf16[1,4,64,256]{3,2,1,0:T(8,128)(2,1)} copy(bf16[1,4,64,256]{3,2,1,0:T(8,128)(2,1)} %get-tuple-element.17) | data formatting | bytes 262144
  29.8 1.9 %copy.25 = f32[256,512]{1,0:T(8,128)} copy(f32[256,512]{1,0:T(8,128)} %get-tuple-element.18) | data formatting | bytes 1048576
  31.7 0.0 copy-done
  31.7 0.6 %copy.26 = f32[512]{0:T(512)} copy(f32[512]{0:T(512)S(1)} %bitcast.6) | data formatting | bytes 4096
Async XLA Ops:
  26.7 5.0 %copy-start = (f32[1,512]{1,0:T(1,128)S(1)}, f32[1,512]{1,0:T(1,128)}, u32[]{:S(2)}) copy-start(f32[1,512]{1,0:T(1,128)} %get-tuple-element.11) | copy-start | bytes 6148

commit v2 on v1

--- a/solution.py
+++ b/solution.py
@@ -13,6 +13,7 @@
 MESH = pl.DeviceIdType.MESH
 F32 = jnp.float32
 BF16 = jnp.bfloat16
+GRANT = 24 << 20
 REACH = 2
 HIGHEST = lax.Precision.HIGHEST
 
@@ -41,14 +42,15 @@
 
 def kernel(
     n, m,
-    steps_ref, ids_ref, gain_ref, bias_ref, tbias_ref, abias_ref,
+    steps_ref, ids_ref, gain_hbm, bias_hbm, tbias_hbm, abias_hbm,
     images_hbm, cot_hbm, first_hbm, second_hbm, tweight_hbm, table_hbm, aweight_hbm,
-    branch_hbm, igrad_hbm, wgrad_hbm, bgrad_ref,
+    branch, igrad, acts_out, pairs_out,
     images, cot, first, second, tweight, table, aweight,
+    gain_ref, bias_ref, tbias_ref, abias_ref,
     wide_first, wide_cot, wide_second, wide_hidden,
-    hidden, gact, nsecond, gpre, nfirst, slope, branch, igrad, wgrad,
+    hidden, gact, nsecond, gpre, nfirst, slope,
     slots, acts, pairs,
-    load_sem, store_sem, halo_send, halo_recv, send_sem, recv_sem,
+    load_sem, halo_send, halo_recv, send_sem, recv_sem,
     act_send, act_recv, pair_send, pair_recv,
 ):
     me = lax.axis_index("tile")
@@ -71,6 +73,10 @@
                 (aweight_hbm, aweight),
                 (first_hbm, first),
                 (second_hbm, second),
+                (gain_hbm, gain_ref),
+                (bias_hbm, bias_ref),
+                (tbias_hbm, tbias_ref),
+                (abias_hbm, abias_ref),
             ]
         )
     ]
@@ -203,7 +209,7 @@
         def _():
             buffer[pl.ds(rows + REACH, REACH)] = jnp.zeros((REACH, cols, channels), BF16)
 
-    for k in (2, 3, 4):
+    for k in (2, 3, 4, 7, 8, 9, 10):
         loads[k].wait()
     half = tweight.shape[0] // 2
     index = lax.broadcasted_iota(jnp.int32, (half, 1), 0).astype(F32)
@@ -288,9 +294,7 @@
         nsecond[at] = normed
         gpre[at] = back
 
-    branch[...] = conv(wide_second, 0, rows, second).astype(BF16).reshape(rows, cols, channels)
-    stores = [pltpu.make_async_copy(branch, branch_hbm.at[0], store_sem.at[0])]
-    stores[0].start()
+    branch[0] = conv(wide_second, 0, rows, second).astype(BF16).reshape(rows, cols, channels)
 
     sums = total(3)
     spread = group_spread(sums * factor, width) / cells
@@ -311,29 +315,12 @@
     for k in range(1, m):
         image_copy(acts, act_send, act_recv, k, True).wait_recv()
         image_copy(pairs, pair_send, pair_recv, k, True).wait_recv()
-    extra = (-m) % 8
-
-    def stacked(pieces):
-        if extra:
-            pieces = pieces + [jnp.zeros((extra, pieces[0].shape[1]), F32)]
-        return jnp.concatenate(pieces, axis=0)
-
-    left = stacked([acts[k] for k in range(m)])
-    for part in range(2):
-        right = stacked([pairs[k][part : part + 1] for k in range(m)])
-        columns = slice(part * channels, (part + 1) * channels)
-        wgrad[:, columns] = lax.dot_general(
-            left, right, (((0,), (0,)), ((), ())), precision=HIGHEST, preferred_element_type=F32
-        )
-        bgrad_ref[:, columns] = jnp.sum(right, axis=0, keepdims=True)
-    stores.append(pltpu.make_async_copy(wgrad, wgrad_hbm, store_sem.at[1]))
-    stores[1].start()
+    acts_out[...] = acts[...]
+    pairs_out[...] = pairs[...]
 
     spread = group_spread(total(4), width) / cells
     result = inverse_first * (back - spread[0:1] - normed * spread[1:2])
-    igrad[...] = result.astype(BF16).reshape(rows, cols, channels)
-    stores.append(pltpu.make_async_copy(igrad, igrad_hbm.at[0], store_sem.at[2]))
-    stores[2].start()
+    igrad[0] = result.astype(BF16).reshape(rows, cols, channels)
 
     for stage in range(5):
         for k in range(1, n):
@@ -351,8 +338,33 @@
         def _():
             halo_copy(which, buffer, False).wait_send()
 
-    for store in stores:
-        store.wait()
+def finish(m, branch_in, igrad_in, acts, pairs, branch_hbm, igrad_hbm, wgrad_hbm, bgrad_ref, wgrad, sem):
+    copies = [
+        pltpu.make_async_copy(branch_in, branch_hbm, sem.at[0]),
+        pltpu.make_async_copy(igrad_in, igrad_hbm, sem.at[1]),
+        pltpu.make_async_copy(wgrad, wgrad_hbm, sem.at[2]),
+    ]
+    copies[0].start()
+    copies[1].start()
+    channels = pairs.shape[2]
+    extra = (-m) % 8
+
+    def stacked(pieces):
+        if extra:
+            pieces = pieces + [jnp.zeros((extra, pieces[0].shape[1]), F32)]
+        return jnp.concatenate(pieces, axis=0)
+
+    left = stacked([acts[k] for k in range(m)])
+    for part in range(2):
+        right = stacked([pairs[k][part : part + 1] for k in range(m)])
+        columns = slice(part * channels, (part + 1) * channels)
+        wgrad[:, columns] = lax.dot_general(
+            left, right, (((0,), (0,)), ((), ())), precision=HIGHEST, preferred_element_type=F32
+        )
+        bgrad_ref[:, columns] = jnp.sum(right, axis=0, keepdims=True)
+    copies[2].start()
+    for copy in copies:
+        copy.wait()
 
 
 def body(
@@ -363,22 +375,22 @@
     count, rows, cols, channels = images.shape
     assert count == 1 and rows >= REACH
     emb = time_weight.shape[1]
-    smem = pl.BlockSpec(memory_space=pltpu.SMEM)
     vmem = pl.BlockSpec(memory_space=pltpu.VMEM)
     anywhere = pl.BlockSpec(memory_space=pl.ANY)
     padded = rows + 2 * REACH
     own, more, most = rows * cols, (rows + 2) * cols, padded * cols
     dma = pltpu.SemaphoreType.DMA
-    branch, igrad, wgrad, bgrad = pl.pallas_call(
+    branch, igrad, acts, pairs = pl.pallas_call(
         functools.partial(kernel, n, m),
         out_shape=(
             jax.ShapeDtypeStruct(images.shape, BF16),
             jax.ShapeDtypeStruct(images.shape, BF16),
-            jax.ShapeDtypeStruct((emb, 2 * channels), F32),
-            jax.ShapeDtypeStruct((1, 2 * channels), F32),
+            jax.ShapeDtypeStruct((m, 1, emb), F32),
+            jax.ShapeDtypeStruct((m, 2, channels), F32),
         ),
-        in_specs=[smem] * 2 + [vmem] * 4 + [anywhere] * 7,
-        out_specs=(anywhere, anywhere, anywhere, vmem),
+        in_specs=[pl.BlockSpec(memory_space=pltpu.SMEM)] * 2
+        + [pl.BlockSpec(memory_space=pltpu.HBM)] * 11,
+        out_specs=(vmem,) * 4,
         scratch_shapes=[
             pltpu.VMEM((padded, cols, channels), BF16),
             pltpu.VMEM((padded, cols, channels), BF16),
@@ -387,6 +399,10 @@
             pltpu.VMEM(time_weight.shape, BF16),
             pltpu.VMEM(class_table.shape, BF16),
             pltpu.VMEM(adaptive_weight.shape, BF16),
+            pltpu.VMEM((1, channels), F32),
+            pltpu.VMEM((1, channels), F32),
+            pltpu.VMEM((1, emb), F32),
+            pltpu.VMEM((1, 2 * channels), F32),
             pltpu.VMEM((most, 3 * channels), BF16),
             pltpu.VMEM((most, 3 * channels), BF16),
             pltpu.VMEM((more, 3 * channels), BF16),
@@ -397,14 +413,10 @@
             pltpu.VMEM((more, channels), F32),
             pltpu.VMEM((own, channels), F32),
             pltpu.VMEM((own, channels), F32),
-            pltpu.VMEM((rows, cols, channels), BF16),
-            pltpu.VMEM((rows, cols, channels), BF16),
-            pltpu.VMEM((emb, 2 * channels), F32),
             pltpu.VMEM((5, n, 2, channels), F32),
             pltpu.VMEM((m, 1, emb), F32),
             pltpu.VMEM((m, 2, channels), F32),
-            dma((7,)),
-            dma((3,)),
+            dma((11,)),
             dma((2, 2)),
             dma((2, 2)),
             dma((5, n)),
@@ -414,12 +426,33 @@
             dma((m,)),
             dma((m,)),
         ],
-        compiler_params=pltpu.CompilerParams(collective_id=0, has_side_effects=True),
+        compiler_params=pltpu.CompilerParams(
+            collective_id=0, has_side_effects=True, vmem_limit_bytes=GRANT
+        ),
     )(
-        timesteps, class_ids, norm_gain[None], norm_bias[None], time_bias[None],
-        adaptive_bias[None], images, cotangent, conv_first, conv_second, time_weight,
-        class_table, adaptive_weight,
+        timesteps, class_ids,
+        *(
+            pltpu.with_memory_space_constraint(operand, pltpu.HBM)
+            for operand in (
+                norm_gain[None], norm_bias[None], time_bias[None],
+                adaptive_bias[None], images, cotangent, conv_first, conv_second, time_weight,
+                class_table, adaptive_weight,
+            )
+        )
     )
+    branch, igrad, wgrad, bgrad = pl.pallas_call(
+        functools.partial(finish, m),
+        out_shape=(
+            jax.ShapeDtypeStruct(images.shape, BF16),
+            jax.ShapeDtypeStruct(images.shape, BF16),
+            jax.ShapeDtypeStruct((emb, 2 * channels), F32),
+            jax.ShapeDtypeStruct((1, 2 * channels), F32),
+        ),
+        in_specs=[anywhere] * 2 + [vmem] * 2,
+        out_specs=(anywhere, anywhere, anywhere, vmem),
+        scratch_shapes=[pltpu.VMEM((emb, 2 * channels), F32), dma((3,))],
+        compiler_params=pltpu.CompilerParams(vmem_limit_bytes=GRANT),
+    )(branch, igrad, acts, pairs)
     return branch, igrad, wgrad, bgrad[0]
 
 

time: 32.5 us -> 27 us (0.83)
  local copies, waits for them, and re-layouts: 5.59 us -> 0 us
    unnamed x6 -> x0, local copies, waits for them, and re-layouts: 5.59 us -> none
    pallas_call x0 -> x1, Pallas kernels: none -> 2.02 us  [body(): pl.pallas_call(functools.partial(finish, m), out_shape=(jax.ShapeDtypeStr...]
    pallas_call x1, Pallas kernels: 24.7 us -> 22.8 us  [body(): pl.pallas_call(functools.partial(kernel, n, m), out_shape=(jax.ShapeDtype...]
where the time goes in v2:
time: 27 us; the launch traced here: 26.8 us
  Pallas kernels  24.9 us (92%)
  between operations  1.93 us (7%)
    pallas_call x1, Pallas kernels, body(): pl.pallas_call(functools.partial(kernel, n, m), out_shape=(jax.ShapeDtype...  22.8 us
    pallas_call x1, Pallas kernels, body(): pl.pallas_call(functools.partial(finish, m), out_shape=(jax.ShapeDtypeStr...  2.02 us

profile of v2, /device:TPU:0, one launch (start us, length us, event | category | flops | bytes accessed | tf_op | source)
XLA Modules:
  0.0 26.8 jit_solution(13484650108147169696)
XLA Ops:
  1.9 22.8 %shard_map.156 = (bf16[1,4,64,256]{3,2,1,0:T(8,128)(2,1)S(1)}, bf16[1,4,64,256]{3,2,1,0:T(8,128)(2,1)S(1)}, f32[4,1,256]{2,1,0:T(1,128)S(1)}, f32[4,2,256]{2,1,0:T(2,128)S(1)}) custom-call(s32[1]{0:T(128)S(6)} %copy.17.steps_ref, s32[1]{0:T(128)S(6)} %copy.18.ids_ref, f32[1,256]{1,0:T(1,128)} %bitcast.6, f32[1,256]{1,0:T(1,128)} %bitcast.7, ...), custom_call_target="tpu_custom_call" | custom-call | tf_op jit(solution)/shard_map/pallas_call | solution.py:383
  24.8 2.0 %shard_map.157 = (bf16[1,4,64,256]{3,2,1,0:T(8,128)(2,1)}, bf16[1,4,64,256]{3,2,1,0:T(8,128)(2,1)}, f32[256,512]{1,0:T(8,128)}, f32[1,512]{1,0:T(1,128)}) custom-call(bf16[1,4,64,256]{3,2,1,0:T(8,128)(2,1)S(1)} %get-tuple-element.12.branch_in, bf16[1,4,64,256]{3,2,1,0:T(8,128)(2,1)S(1)} %get-tuple-element.13.igrad_in, ...), custom_call_target="tpu_custom_call" | custom-call | tf_op jit(solution)/shard_map/pallas_call | solution.py:443

commit v3 on v2

--- a/solution.py
+++ b/solution.py
@@ -44,7 +44,7 @@
     n, m,
     steps_ref, ids_ref, gain_hbm, bias_hbm, tbias_hbm, abias_hbm,
     images_hbm, cot_hbm, first_hbm, second_hbm, tweight_hbm, table_hbm, aweight_hbm,
-    branch, igrad, acts_out, pairs_out,
+    branch, igrad, wgrad, bgrad,
     images, cot, first, second, tweight, table, aweight,
     gain_ref, bias_ref, tbias_ref, abias_ref,
     wide_first, wide_cot, wide_second, wide_hidden,
@@ -188,10 +188,9 @@
     loads[0].wait()
     values = flat(images, REACH, rows)
     sums = column_sums(values, values * values)
-    loads[1].wait()
     pl.semaphore_wait(barrier, n - 1 + m - 1)
     share(0, sums)
-    for which, buffer in enumerate((images, cot)):
+    def halo_start(which, buffer):
 
         @pl.when(above)
         def _():
@@ -208,6 +207,8 @@
         @pl.when(jnp.logical_not(below))
         def _():
             buffer[pl.ds(rows + REACH, REACH)] = jnp.zeros((REACH, cols, channels), BF16)
+
+    halo_start(0, images)
 
     for k in (2, 3, 4, 7, 8, 9, 10):
         loads[k].wait()
@@ -234,6 +235,9 @@
     )[0:1]
     share(1, jnp.concatenate([partial[:, :channels], partial[:, channels:]], axis=0))
 
+    loads[1].wait()
+    halo_start(1, cot)
+
     gain, bias = gain_ref[...], bias_ref[...]
     centre, inverse_first = moments(total(0))
 
@@ -315,8 +319,21 @@
     for k in range(1, m):
         image_copy(acts, act_send, act_recv, k, True).wait_recv()
         image_copy(pairs, pair_send, pair_recv, k, True).wait_recv()
-    acts_out[...] = acts[...]
-    pairs_out[...] = pairs[...]
+    extra = (-m) % 8
+
+    def stacked(pieces):
+        if extra:
+            pieces = pieces + [jnp.zeros((extra, pieces[0].shape[1]), F32)]
+        return jnp.concatenate(pieces, axis=0)
+
+    left = stacked([acts[k] for k in range(m)])
+    for part in range(2):
+        right = stacked([pairs[k][part : part + 1] for k in range(m)])
+        columns = slice(part * channels, (part + 1) * channels)
+        wgrad[:, columns] = lax.dot_general(
+            left, right, (((0,), (0,)), ((), ())), precision=HIGHEST, preferred_element_type=F32
+        )
+        bgrad[:, columns] = jnp.sum(right, axis=0, keepdims=True)
 
     spread = group_spread(total(4), width) / cells
     result = inverse_first * (back - spread[0:1] - normed * spread[1:2])
@@ -338,31 +355,14 @@
         def _():
             halo_copy(which, buffer, False).wait_send()
 
-def finish(m, branch_in, igrad_in, acts, pairs, branch_hbm, igrad_hbm, wgrad_hbm, bgrad_ref, wgrad, sem):
+def finish(*refs):
+    count = (len(refs) - 1) // 2
+    sem = refs[-1]
     copies = [
-        pltpu.make_async_copy(branch_in, branch_hbm, sem.at[0]),
-        pltpu.make_async_copy(igrad_in, igrad_hbm, sem.at[1]),
-        pltpu.make_async_copy(wgrad, wgrad_hbm, sem.at[2]),
+        pltpu.make_async_copy(refs[k], refs[count + k], sem.at[k]) for k in range(count)
     ]
-    copies[0].start()
-    copies[1].start()
-    channels = pairs.shape[2]
-    extra = (-m) % 8
-
-    def stacked(pieces):
-        if extra:
-            pieces = pieces + [jnp.zeros((extra, pieces[0].shape[1]), F32)]
-        return jnp.concatenate(pieces, axis=0)
-
-    left = stacked([acts[k] for k in range(m)])
-    for part in range(2):
-        right = stacked([pairs[k][part : part + 1] for k in range(m)])
-        columns = slice(part * channels, (part + 1) * channels)
-        wgrad[:, columns] = lax.dot_general(
-            left, right, (((0,), (0,)), ((), ())), precision=HIGHEST, preferred_element_type=F32
-        )
-        bgrad_ref[:, columns] = jnp.sum(right, axis=0, keepdims=True)
-    copies[2].start()
+    for copy in copies:
+        copy.start()
     for copy in copies:
         copy.wait()
 
@@ -380,13 +380,13 @@
     padded = rows + 2 * REACH
     own, more, most = rows * cols, (rows + 2) * cols, padded * cols
     dma = pltpu.SemaphoreType.DMA
-    branch, igrad, acts, pairs = pl.pallas_call(
+    results = pl.pallas_call(
         functools.partial(kernel, n, m),
         out_shape=(
             jax.ShapeDtypeStruct(images.shape, BF16),
             jax.ShapeDtypeStruct(images.shape, BF16),
-            jax.ShapeDtypeStruct((m, 1, emb), F32),
-            jax.ShapeDtypeStruct((m, 2, channels), F32),
+            jax.ShapeDtypeStruct((emb, 2 * channels), F32),
+            jax.ShapeDtypeStruct((1, 2 * channels), F32),
         ),
         in_specs=[pl.BlockSpec(memory_space=pltpu.SMEM)] * 2
         + [pl.BlockSpec(memory_space=pltpu.HBM)] * 11,
@@ -441,18 +441,13 @@
         )
     )
     branch, igrad, wgrad, bgrad = pl.pallas_call(
-        functools.partial(finish, m),
-        out_shape=(
-            jax.ShapeDtypeStruct(images.shape, BF16),
-            jax.ShapeDtypeStruct(images.shape, BF16),
-            jax.ShapeDtypeStruct((emb, 2 * channels), F32),
-            jax.ShapeDtypeStruct((1, 2 * channels), F32),
-        ),
-        in_specs=[anywhere] * 2 + [vmem] * 2,
-        out_specs=(anywhere, anywhere, anywhere, vmem),
-        scratch_shapes=[pltpu.VMEM((emb, 2 * channels), F32), dma((3,))],
+        finish,
+        out_shape=tuple(jax.ShapeDtypeStruct(r.shape, r.dtype) for r in results),
+        in_specs=[anywhere] * 4,
+        out_specs=(anywhere,) * 4,
+        scratch_shapes=[dma((4,))],
         compiler_params=pltpu.CompilerParams(vmem_limit_bytes=GRANT),
-    )(branch, igrad, acts, pairs)
+    )(*results)
     return branch, igrad, wgrad, bgrad[0]
 
 

time: 27 us -> 25.9 us (0.959)
  Pallas kernels: 24.9 us -> 23.8 us
    pallas_call x1, Pallas kernels: 2.02 us -> 0.92 us  [body(): pl.pallas_call(finish, out_shape=tuple((jax.ShapeDtypeStruct(r.shape, r.d...]
where the time goes in v3:
time: 25.9 us; the launch traced here: 25.7 us
  Pallas kernels  23.8 us (92%)
  between operations  1.93 us (7%)
    pallas_call x1, Pallas kernels, body(): pl.pallas_call(functools.partial(kernel, n, m), out_shape=(jax.ShapeDtype...  22.9 us
    pallas_call x1, Pallas kernels, body(): pl.pallas_call(finish, out_shape=tuple((jax.ShapeDtypeStruct(r.shape, r.d...  0.92 us

profile of v3, /device:TPU:0, one launch (start us, length us, event | category | flops | bytes accessed | tf_op | source)
XLA Modules:
  0.0 25.7 jit_solution(10996030201594590553)
XLA Ops:
  1.9 22.9 %shard_map.156 = (bf16[1,4,64,256]{3,2,1,0:T(8,128)(2,1)S(1)}, bf16[1,4,64,256]{3,2,1,0:T(8,128)(2,1)S(1)}, f32[256,512]{1,0:T(8,128)S(1)}, f32[1,512]{1,0:T(1,128)S(1)}) custom-call(s32[1]{0:T(128)S(6)} %copy.17.steps_ref, s32[1]{0:T(128)S(6)} %copy.18.ids_ref, f32[1,256]{1,0:T(1,128)} %bitcast.6, f32[1,256]{1,0:T(1,128)} %bitcast.7, f32[1,256]{1,0:T(1,128)} %bitcast.8, ...), custom_call_target="tpu_custom_call" | custom-call | tf_op jit(solution)/shard_map/pallas_call | solution.py:383
  24.8 0.9 %shard_map.157 = (bf16[1,4,64,256]{3,2,1,0:T(8,128)(2,1)}, bf16[1,4,64,256]{3,2,1,0:T(8,128)(2,1)}, f32[256,512]{1,0:T(8,128)}, f32[1,512]{1,0:T(1,128)}) custom-call(bf16[1,4,64,256]{3,2,1,0:T(8,128)(2,1)S(1)} %get-tuple-element.12.refs_0_, bf16[1,4,64,256]{3,2,1,0:T(8,128)(2,1)S(1)} %get-tuple-element.13.refs_1_, ...), custom_call_target="tpu_custom_call" | custom-call | tf_op jit(solution)/shard_map/pallas_call | solution.py:443
